TPU v7x, 32 devices: a whole 2x2x4 slice. The times are simulated.
32 devices in a mesh: tm: 2 (over core), height: 8 (over z, y), head: 2 (over x).
Axes of the slice: x: 2, y: 2, z: 4, core: 2. Of those that a mesh axis runs over, the one named last changes fastest.
Arguments:
- queries: bfloat16 [4, 16, 64, 1280], P('tm', 'height', None, 'head'), may hold values from -22 to 22
- keys_values: bfloat16 [2, 4, 16, 64, 1280], P(None, 'tm', 'height', None, 'head'), may hold values from -7 to 7
- out_weight: bfloat16 [1280, 5120], P('head'), may hold values from -0.15625 to 0.15625
Outputs:
- mixed: bfloat16 [64, 4, 16, 5120], P('head', 'tm', 'height')
All inputs are finite; a program needn't handle non-finite values.
Results may differ from a plain program's by a relative error of at most 0.013.
Values may be sent and summed in bfloat16 or wider, within the bound.
A program may use at most 128 MiB of HBM per device.

v0:
```python
import math
import jax
import jax.numpy as jnp
from jax import lax
from jax.sharding import PartitionSpec as P

HD = 128
TILE = 16
WINDOW = 3
PAD_ROWS = 2
VALID_COLS = 52
masked_value = -1e30


def from_partner(value, axis, apart):
    mask = 2**apart
    pairs = [(source, source ^ mask) for source in range(lax.axis_size(axis))]
    return lax.ppermute(value, axis, pairs)


def window_start(tile_index, tile_count):
    span_size = min(tile_count, WINDOW)
    return (jnp.clip(tile_index - 1, 0, tile_count - span_size), span_size)


def column_groups(col_tiles):
    col_span = min(col_tiles, WINDOW)
    grouped = []
    for col_tile in range(col_tiles):
        key_begin = max(0, min(col_tile - 1, col_tiles - col_span))
        if len(grouped) > 0 and grouped[-1][2] == key_begin:
            grouped[-1] = (grouped[-1][0], col_tile + 1, key_begin)
        else:
            grouped.append((col_tile, col_tile + 1, key_begin))
    return (grouped, col_span)


def edge_frame(local_keys, side_index):
    last_frame = local_keys.shape[1] - 1
    begin = (1 - side_index) * last_frame
    return lax.dynamic_slice_in_dim(local_keys, begin, 1, 1)


def attach_rim(local_keys, rim_frame, side_index):
    joined = jnp.concatenate([rim_frame, local_keys, rim_frame], axis=1)
    begin = 1 - side_index
    return lax.dynamic_slice_in_dim(joined, begin, local_keys.shape[1] + 1, 1)


def on_device(queries, keys_values, out_weight):
    frames_dev, rows_dev, col_count, width_dev = queries.shape
    heads_dev = width_dev // HD
    frame_count = frames_dev * lax.axis_size("tm")
    frame_rows = rows_dev * lax.axis_size("height")
    valid_rows = frame_rows - PAD_ROWS
    row_tiles = frame_rows // TILE
    side_index = lax.axis_index("tm")
    first_frame = side_index * frames_dev
    first_row = lax.axis_index("height") * rows_dev
    score_scale = 1.0 / math.sqrt(HD)
    query_frames = first_frame + jnp.arange(frames_dev, dtype=jnp.int32)
    frame_low, frame_span = window_start(query_frames, frame_count)
    query_rows = first_row + jnp.arange(rows_dev, dtype=jnp.int32)
    row_tile_low, row_span = window_start(query_rows // TILE, row_tiles)
    row_low = row_tile_low * TILE
    row_high = row_low + row_span * TILE
    grouped, col_span = column_groups(col_count // TILE)
    key_width = col_span * TILE
    query_groups = []
    col_fits = []
    starters = []
    for first_tile, last_tile, key_tile in grouped:
        selected = queries[:, :, first_tile * TILE : last_tile * TILE, :]
        query_groups.append(selected.reshape(-1, width_dev))
        col_fits.append(key_tile * TILE + jnp.arange(key_width, dtype=jnp.int32) < VALID_COLS)
        query_total = selected.shape[0] * selected.shape[1] * selected.shape[2]
        starters.append(
            tuple(
                (
                    (
                        jnp.full((query_total,), masked_value, jnp.float32),
                        jnp.zeros((query_total,), jnp.float32),
                        jnp.zeros((query_total, HD), jnp.float32),
                    )
                    for member in range(heads_dev)
                )
            )
        )
    initial = tuple(starters)
    whole_rows = lax.all_gather(keys_values, "height", axis=2, tiled=True)
    rim_frame = from_partner(edge_frame(whole_rows, side_index), "tm", 0)
    with_rims = attach_rim(whole_rows, rim_frame, side_index)
    extended = with_rims.shape[1]
    row_piece = with_rims.shape[2]
    key_frames = first_frame - side_index + jnp.arange(extended, dtype=jnp.int32)
    key_rows = jnp.arange(row_piece, dtype=jnp.int32)
    time_fits = (key_frames[None, :] >= frame_low[:, None]) & (
        key_frames[None, :] < frame_low[:, None] + frame_span
    )
    row_fits = (key_rows[None, :] >= row_low[:, None]) & (key_rows[None, :] < row_high[:, None])
    row_fits = row_fits & (key_rows[None, :] < valid_rows)
    updated = []
    for add_group_id, (add_first_tile, add_last_tile, add_key_tile) in enumerate(grouped):
        add_query_cols = (add_last_tile - add_first_tile) * TILE
        visible = (
            time_fits[:, None, None, :, None, None]
            & row_fits[None, :, None, None, :, None]
            & col_fits[add_group_id][None, None, None, None, None, :]
        )
        visible = jnp.broadcast_to(
            visible, (frames_dev, rows_dev, add_query_cols, extended, row_piece, key_width)
        )
        visible = visible.reshape(
            frames_dev * rows_dev * add_query_cols, extended * row_piece * key_width
        )
        col_begin = add_key_tile * TILE
        key_block = with_rims[0, :, :, col_begin : col_begin + key_width, :].reshape(-1, width_dev)
        value_block = with_rims[1, :, :, col_begin : col_begin + key_width, :].reshape(
            -1, width_dev
        )
        head_states = []
        for member in range(heads_dev):
            running_max, running_sum, running_out = initial[add_group_id][member]
            head_query = query_groups[add_group_id][:, member * HD : (member + 1) * HD]
            head_keys = key_block[:, member * HD : (member + 1) * HD]
            head_values = value_block[:, member * HD : (member + 1) * HD]
            scores = (
                jnp.einsum("qd,kd->qk", head_query, head_keys, preferred_element_type=jnp.float32)
                * score_scale
            )
            scores = jnp.where(visible, scores, masked_value)
            new_max = jnp.maximum(running_max, jnp.max(scores, axis=1))
            weights = jnp.where(visible, jnp.exp(scores - new_max[:, None]), 0.0)
            new_sum = jnp.sum(weights, axis=1)
            new_out = jnp.dot(
                weights.astype(jnp.bfloat16), head_values, preferred_element_type=jnp.float32
            )
            head_states.append((new_max, new_sum, new_out))
        updated.append(tuple(head_states))
    final_state = tuple(updated)
    pieces = []
    for group_id, (first_tile, last_tile, key_tile) in enumerate(grouped):
        query_cols = (last_tile - first_tile) * TILE
        head_parts = [state[2] / state[1][:, None] for state in final_state[group_id]]
        group_out = jnp.concatenate(head_parts, axis=1).astype(jnp.bfloat16)
        group_out = group_out.reshape(frames_dev, rows_dev, query_cols, width_dev)
        pieces.append(jnp.transpose(group_out, (2, 0, 1, 3)))
    attended = jnp.concatenate(pieces, axis=0)
    return lax.psum_scatter(
        jnp.einsum(
            "cfrh,hd->cfrd", attended, out_weight, preferred_element_type=jnp.float32
        ).astype(jnp.bfloat16),
        "head",
        scatter_dimension=0,
        tiled=True,
    )


def solution(mesh):
    placed = (
        P("tm", "height", None, "head"),
        P(None, "tm", "height", None, "head"),
        P("head", None),
    )
    return jax.shard_map(
        on_device,
        mesh=mesh,
        in_specs=placed,
        out_specs=P("head", "tm", "height", None),
        check_vma=False,
    )
```

profile of v0, /device:TPU:0, one launch (start us, length us, event | category | flops | bytes accessed | tf_op | source)
XLA Modules:
  0.0 177.9 jit_solution(4382157549609009276)
XLA Ops:
  6.5 0.7 all-gather.2.cloned.1.call-update
  7.3 0.0 reduce-scatter.2.cloned.1.call-start
  7.3 91.2 %all-gather.2.cloned.1.call-done = bf16[2,2,16,64,640]{4,3,2,1,0:T(8,128)(2,1)} async-done(((bf16[2,2,2,64,640]{4,3,2,1,0:T(8,128)(2,1)}), bf16[2,2,16,64,640]{4,3,2,1,0:T(8,128)(2,1)}) %all-gather.2.cloned.1.call-update) | async-done | bytes 5242896 | tf_op jit(solution)/shard_map/all_gather | solution.py:90
  98.6 3.5 %constant_dynamic-slice_fusion = bf16[2,1,16,64,640]{4,3,2,1,0:T(8,128)(2,1)} fusion(bf16[2,2,16,64,640]{4,3,2,1,0:T(8,128)(2,1)} %all-gather.2.cloned.1.call-done, s32[]{:T(128)S(6)} %select_n.80), kind=kLoop, calls=%fused_computation.160 | loop fusion | bytes 5242884 | tf_op jit(solution)/shard_map/dynamic_slice | solution.py:41
  102.1 0.0 collective-permute-start
  102.2 0.1 compare_and_fusion
  102.2 0.1 and_and_fusion
  102.3 0.1 broadcast_and_fusion.2
  102.4 0.1 broadcast_and_fusion.1
  102.5 0.2 broadcast_in_dim.29
  102.7 1.5 reshape.255
  104.2 0.4 copy.6
  104.6 0.0 copy-start
  104.6 0.2 broadcast_in_dim.32
  104.8 1.5 reshape.257
  106.4 0.4 copy.16
  106.8 0.5 collective-permute-done
  107.3 5.7 %fusion.1 = bf16[2,3,16,64,640]{4,3,2,1,0:T(8,128)(2,1)S(1)} fusion(s32[]{:T(128)S(6)} %select_n.81, bf16[2,1,16,64,640]{4,3,2,1,0:T(8,128)(2,1)} %collective-permute-done, bf16[2,2,16,64,640]{4,3,2,1,0:T(8,128)(2,1)} %all-gather.2.cloned.1.call-done), kind=kLoop, calls=%fused_computation.4 | loop fusion | flops 7864320 | bytes 15728644 | tf_op jit(solution)/shard_map/concatenate | solution.py:45
  113.1 1.7 fusion.131
  114.8 0.5 fusion.139
  115.3 0.5 fusion.140
  115.8 0.5 fusion.141
  116.2 0.5 fusion.142
  116.7 0.5 fusion.138
  117.2 0.5 fusion.134
  117.7 0.5 fusion.135
  118.2 0.5 fusion.136
  118.7 0.5 fusion.137
  119.2 0.5 fusion.133
  119.7 1.1 fusion.45
  120.8 0.5 fusion.31
  121.3 0.5 fusion.30
  121.7 0.5 fusion.29
  122.2 0.5 fusion.28
  122.7 0.5 fusion.27
  123.2 1.1 fusion.55
  124.3 0.0 slice-start
  124.3 0.5 fusion.36
  124.8 0.5 fusion.35
  125.2 0.0 slice-start.1
  125.3 0.5 fusion.34
  125.7 0.5 fusion.33
  126.2 0.5 fusion.32
  126.9 0.6 slice-done.1
  127.5 3.8 %fusion.4 = bf16[64,2,2,5120]{3,0,2,1:T(8,128)(2,1)} fusion(bf16[640,5120]{1,0:T(8,128)(2,1)S(1)} %bitcast.112, bf16[32,2,2,640]{3,0,2,1:T(8,128)(2,1)S(1)} %bitcast.110, bf16[32,2,2,640]{3,0,2,1:T(8,128)(2,1)S(1)} %bitcast.109), kind=kOutput, calls=%fused_computation.7 | convolution fusion | flops 1679687680 | bytes 9502720 | tf_op jit(solution)/shard_map/cfrh,hd->cfrd/dot_general | solution.py:150
  131.2 0.0 reduce-scatter.2.cloned.1.call-update
  131.2 36.1 %reduce-scatter.2.cloned.1.call-done = bf16[32,2,2,5120]{3,0,2,1:T(8,128)(2,1)} async-done(((bf16[64,2,2,5120]{3,0,2,1:T(8,128)(2,1)}), bf16[32,2,2,5120]{3,0,2,1:T(8,128)(2,1)}) %reduce-scatter.2.cloned.1.call-update) | async-done | bytes 1310736 | tf_op jit(solution)/shard_map/reduce_scatter | solution.py:149
  167.4 3.7 %copy.25 = bf16[32,2,2,5120]{3,2,1,0:T(2,128)(2,1)} copy(bf16[32,2,2,5120]{3,0,2,1:T(8,128)(2,1)} %reduce-scatter.2.cloned.1.call-done) | data formatting | bytes 2621440 | tf_op jit(solution)/shard_map/reduce_scatter | solution.py:149
  (30 shorter events, 0.2 us)
Async XLA Ops:
  6.5 92.0 %all-gather.2.cloned.1.call-start = ((), (), s32[]{:S(2)}) async-start(), calls=%async_computation.1 | async-start | bytes 5898240 | tf_op jit(solution)/shard_map/all_gather | solution.py:90
  7.3 160.1 %reduce-scatter.2.cloned.1.call-start = ((), (), s32[]{:S(2)}) async-start(), calls=%async_computation.2 | async-start | bytes 3932160 | tf_op jit(solution)/shard_map/reduce_scatter | solution.py:149
  102.1 5.3 %collective-permute-start = (bf16[2,1,16,64,640]{4,3,2,1,0:T(8,128)(2,1)}, bf16[2,1,16,64,640]{4,3,2,1,0:T(8,128)(2,1)}, u32[]{:S(2)}, u32[]{:S(2)}) collective-permute-start(bf16[2,1,16,64,640]{4,3,2,1,0:T(8,128)(2,1)} %constant_dynamic-slice_fusion), channel_id=1, source_target_pairs={{0,16},{16,0},{1,17},{17,1},{2,18},{18,2},{3,19},{19,3},{4,20},{20... | collective-permute-start | bytes 7864328 | tf_op jit(solution)/shard_map/ppermute | solution.py:18
  104.6 2.1 %copy-start = (bf16[2,2,64,640]{3,2,1,0:T(8,128)(2,1)S(1)}, bf16[2,2,64,640]{3,2,1,0:T(8,128)(2,1)}, u32[]{:S(2)}) copy-start(bf16[2,2,64,640]{3,2,1,0:T(8,128)(2,1)} %param.3) | copy-start | bytes 983044
  124.3 2.6 %slice-start = ((s8[6553600]{0:T(1024)(128)(4,1)}), s8[4194304]{0:T(1024)(128)(4,1)S(1)}, s32[]{:S(2)}) async-start(s8[6553600]{0:T(1024)(128)(4,1)} %bitcast.111), calls=%async_computation.3 | async-start | bytes 8388608
  125.2 2.2 %slice-start.1 = ((s8[6553600]{0:T(1024)(128)(4,1)}), s8[2359296]{0:T(1024)(128)(4,1)S(1)}, s32[]{:S(2)}) async-start(s8[6553600]{0:T(1024)(128)(4,1)} %bitcast.111), calls=%async_computation.4 | async-start | bytes 4718592
Sparse Core Ops, SparseCore 0:
  9.5 88.9 all-gather.1
  131.4 35.9 reduce-scatter.1
where the time goes:
time: 178 us
  waiting for transfers between devices  129 us (72%)
  local copies, waits for them, and re-layouts  13.9 us (8%)
  between operations  13.7 us (8%)
  matrix products  13.4 us (8%)
  other arithmetic  8.24 us (5%)
    all_gather x1, waiting for transfers between devices, on_device(): whole_rows = lax.all_gather(keys_values, 'height', axis=2, tiled=True)  91.2 us
    reduce_scatter x1, waiting for transfers between devices, on_device(): lax.psum_scatter(jnp.einsum('cfrh,hd->cfrd', attended, out_weight, prefer...  36.1 us
    concatenate x1, other arithmetic, attach_rim(): joined = jnp.concatenate([rim_frame, local_keys, rim_frame], axis=1)  5.71 us
    dot_general x10, matrix products, on_device(): jnp.einsum('qd,kd->qk', head_query, head_keys, preferred_element_type=jnp...  4.89 us
    dot_general x10, matrix products, on_device(): jnp.dot(weights.astype(jnp.bfloat16), head_values, preferred_element_type...  4.72 us
    reshape x4, local copies, waits for them, and re-layouts, on_device(): visible.reshape(frames_dev * rows_dev * add_query_cols, extended * row_pi...  3.79 us
    dot_general x1, matrix products, on_device(): jnp.einsum('cfrh,hd->cfrd', attended, out_weight, preferred_element_type=...  3.77 us
    reduce_scatter x1, local copies, waits for them, and re-layouts, on_device(): lax.psum_scatter(jnp.einsum('cfrh,hd->cfrd', attended, out_weight, prefer...  3.72 us
  transfers between devices with their start and end apart: 3, of which 3 were waited for; matrix products, arithmetic and copies ran while one was open for 3% of the time, Pallas kernels for 0%

commit v1 on v0

--- a/solution.py
+++ b/solution.py
@@ -87,7 +87,14 @@
             )
         )
     initial = tuple(starters)
-    whole_rows = lax.all_gather(keys_values, "height", axis=2, tiled=True)
+    ways, here = (lax.axis_size("height"), lax.axis_index("height"))
+    whole_rows, reach = (keys_values, 1)
+    while reach < ways:
+        theirs = lax.ppermute(whole_rows, "height", [(d, d ^ reach) for d in range(ways)])
+        mine_first = jnp.concatenate([whole_rows, theirs], axis=2)
+        theirs_first = jnp.concatenate([theirs, whole_rows], axis=2)
+        whole_rows = jnp.where(here & reach == 0, mine_first, theirs_first)
+        reach = 2 * reach
     rim_frame = from_partner(edge_frame(whole_rows, side_index), "tm", 0)
     with_rims = attach_rim(whole_rows, rim_frame, side_index)
     extended = with_rims.shape[1]

time: 178 us -> 259 us (1.46)
  waiting for transfers between devices: 129 us -> 194 us
  other arithmetic: 8.24 us -> 16.8 us
  starting transfers between devices: 0.04 us -> 7.4 us
    ppermute x0 -> x3, waiting for transfers between devices: none -> 155 us  [on_device(): lax.ppermute(whole_rows, 'height', [(d, d ^ reach) for d in range(ways)])]
    all_gather x1 -> x0, waiting for transfers between devices: 91.2 us -> none  [on_device(): whole_rows = lax.all_gather(keys_values, 'height', axis=2, tiled=True)]
    select_n x0 -> x3, other arithmetic: none -> 8.53 us  [on_device(): whole_rows = jnp.where(here & reach == 0, mine_first, theirs_first)]
    ppermute x0 -> x3, starting transfers between devices: none -> 7.39 us  [on_device(): lax.ppermute(whole_rows, 'height', [(d, d ^ reach) for d in range(ways)])]
  transfers between devices with their start and end apart: 3 -> 5, of which waited for: 3 -> 5; matrix products, arithmetic and copies ran while one was open for 3% -> 2% of each run, Pallas kernels for 0% -> 0%
where the time goes in v1:
time: 259 us
  waiting for transfers between devices  194 us (75%)
  other arithmetic  16.8 us (6%)
  between operations  13.7 us (5%)
  local copies, waits for them, and re-layouts  13.6 us (5%)
  matrix products  13.4 us (5%)
  starting transfers between devices  7.4 us (3%)
    ppermute x3, waiting for transfers between devices, on_device(): lax.ppermute(whole_rows, 'height', [(d, d ^ reach) for d in range(ways)])  155 us
    reduce_scatter x1, waiting for transfers between devices, on_device(): lax.psum_scatter(jnp.einsum('cfrh,hd->cfrd', attended, out_weight, prefer...  38.7 us
    select_n x3, other arithmetic, on_device(): whole_rows = jnp.where(here & reach == 0, mine_first, theirs_first)  8.53 us
    ppermute x3, starting transfers between devices, on_device(): lax.ppermute(whole_rows, 'height', [(d, d ^ reach) for d in range(ways)])  7.39 us
    concatenate x1, other arithmetic, attach_rim(): joined = jnp.concatenate([rim_frame, local_keys, rim_frame], axis=1)  5.71 us
  transfers between devices with their start and end apart: 5, of which 5 were waited for; matrix products, arithmetic and copies ran while one was open for 2% of the time, Pallas kernels for 0%

profile of v1, /device:TPU:0, one launch (start us, length us, event | category | flops | bytes accessed | tf_op | source)
XLA Modules:
  0.0 259.1 jit_solution(15216205606600074109)
XLA Ops:
  6.5 3.0 %collective-permute-start = (bf16[2,2,2,64,640]{4,3,2,1,0:T(8,128)(2,1)}, bf16[2,2,2,64,640]{4,3,2,1,0:T(8,128)(2,1)S(1)}, u32[]{:S(2)}, u32[]{:S(2)}) collective-permute-start(bf16[2,2,2,64,640]{4,3,2,1,0:T(8,128)(2,1)} %param.4), channel_id=1, source_target_pairs={{0,2},{2,0},{4,6},{6,4},{8,10},{10,8},{12,14},{14,12},{1,3},{3,1},... | collective-permute-start | bytes 1966088 | tf_op jit(solution)/shard_map/ppermute | solution.py:93
  9.5 14.9 %collective-permute-done = bf16[2,2,2,64,640]{4,3,2,1,0:T(8,128)(2,1)S(1)} collective-permute-done((bf16[2,2,2,64,640]{4,3,2,1,0:T(8,128)(2,1)}, bf16[2,2,2,64,640]{4,3,2,1,0:T(8,128)(2,1)S(1)}, u32[]{:S(2)}, u32[]{:S(2)}) %collective-permute-start) | collective-permute-done | bytes 655392 | tf_op jit(solution)/shard_map/ppermute | solution.py:93
  24.4 1.5 maximum_select_fusion.2
  26.0 1.9 collective-permute-start.1
  27.9 28.3 %collective-permute-done.1 = bf16[2,2,4,64,640]{4,3,2,1,0:T(8,128)(2,1)} collective-permute-done((bf16[2,2,4,64,640]{4,3,2,1,0:T(8,128)(2,1)S(1)}, bf16[2,2,4,64,640]{4,3,2,1,0:T(8,128)(2,1)}, u32[]{:S(2)}, u32[]{:S(2)}) %collective-permute-start.1) | collective-permute-done | bytes 1310752 | tf_op jit(solution)/shard_map/ppermute | solution.py:93
  56.1 2.9 %maximum_select_fusion.1 = bf16[2,2,8,64,640]{4,3,2,1,0:T(8,128)(2,1)S(1)} fusion(bf16[2,2,4,64,640]{4,3,2,1,0:T(8,128)(2,1)} %collective-permute-done.1, bf16[2,2,4,64,640]{4,3,2,1,0:T(8,128)(2,1)} %copy-done.1, pred[]{:T(512)S(6)} %eq.10), kind=kLoop, calls=%fused_computation.39 | loop fusion | flops 3932160 | bytes 5242881 | tf_op jit(solution)/shard_map/jit(_where)/select_n | solution.py:96
  59.1 2.6 collective-permute-start.2
  61.6 111.8 %collective-permute-done.2 = bf16[2,2,8,64,640]{4,3,2,1,0:T(8,128)(2,1)} collective-permute-done((bf16[2,2,8,64,640]{4,3,2,1,0:T(8,128)(2,1)S(1)}, bf16[2,2,8,64,640]{4,3,2,1,0:T(8,128)(2,1)}, u32[]{:S(2)}, u32[]{:S(2)}) %collective-permute-start.2) | collective-permute-done | bytes 2621472 | tf_op jit(solution)/shard_map/ppermute | solution.py:93
  173.5 4.1 %maximum_select_fusion = bf16[2,2,16,64,640]{4,3,2,1,0:T(8,128)(2,1)S(1)} fusion(bf16[2,2,8,64,640]{4,3,2,1,0:T(8,128)(2,1)} %collective-permute-done.2, bf16[2,2,8,64,640]{4,3,2,1,0:T(8,128)(2,1)S(1)} %maximum_select_fusion.1, pred[]{:T(512)S(6)} %eq.9), kind=kLoop, calls=%fused_computation.8 | loop fusion | flops 7864320 | bytes 10485761 | tf_op jit(solution)/shard_map/jit(_where)/select_n | solution.py:96
  177.5 2.0 constant_dynamic-slice_fusion
  179.5 1.3 copy-done
  181.0 0.1 broadcast_and_fusion.2
  181.0 0.1 broadcast_and_fusion.1
  181.2 0.2 broadcast_in_dim.29
  181.4 1.5 reshape.255
  182.9 0.4 copy.6
  183.3 0.2 broadcast_in_dim.32
  183.5 1.5 reshape.257
  185.0 0.4 copy.16
  185.5 0.5 collective-permute-done.3
  186.0 5.7 %fusion.1 = bf16[2,3,16,64,640]{4,3,2,1,0:T(8,128)(2,1)S(1)} fusion(s32[]{:T(128)S(6)} %select_n.111, bf16[2,1,16,64,640]{4,3,2,1,0:T(8,128)(2,1)} %collective-permute-done.3, bf16[2,2,16,64,640]{4,3,2,1,0:T(8,128)(2,1)} %copy-done), kind=kLoop, calls=%fused_computation.4 | loop fusion | flops 7864320 | bytes 15728644 | tf_op jit(solution)/shard_map/concatenate | solution.py:45
  191.7 1.7 fusion.131
  193.4 0.5 fusion.139
  193.9 0.5 fusion.140
  194.4 0.5 fusion.141
  194.9 0.5 fusion.142
  195.4 0.5 fusion.138
  195.9 0.5 fusion.135
  196.4 0.5 fusion.136
  196.9 0.5 fusion.137
  197.4 0.5 fusion.134
  197.9 0.5 fusion.133
  198.4 1.1 fusion.45
  199.5 0.5 fusion.31
  199.9 0.5 fusion.30
  200.4 0.5 fusion.29
  200.9 0.5 fusion.28
  201.3 0.5 fusion.27
  201.9 1.1 fusion.55
  203.0 0.5 fusion.36
  203.4 0.5 fusion.35
  203.9 0.5 fusion.34
  204.4 0.5 fusion.33
  204.9 0.5 fusion.32
  205.5 0.6 slice-done.1
  206.1 3.8 %fusion.4 = bf16[64,2,2,5120]{3,0,2,1:T(8,128)(2,1)} fusion(bf16[640,5120]{1,0:T(8,128)(2,1)S(1)} %bitcast.112, bf16[32,2,2,640]{3,0,2,1:T(8,128)(2,1)S(1)} %bitcast.110, bf16[32,2,2,640]{3,0,2,1:T(8,128)(2,1)S(1)} %bitcast.109), kind=kOutput, calls=%fused_computation.7 | convolution fusion | flops 1679687680 | bytes 9502720 | tf_op jit(solution)/shard_map/cfrh,hd->cfrd/dot_general | solution.py:157
  209.9 38.7 %reduce-scatter.2.cloned.1.call-done = bf16[32,2,2,5120]{3,0,2,1:T(8,128)(2,1)} async-done(((bf16[64,2,2,5120]{3,0,2,1:T(8,128)(2,1)}), bf16[32,2,2,5120]{3,0,2,1:T(8,128)(2,1)}) %reduce-scatter.2.cloned.1.call-update) | async-done | bytes 1310736 | tf_op jit(solution)/shard_map/reduce_scatter | solution.py:156
  248.6 3.7 %copy.25 = bf16[32,2,2,5120]{3,2,1,0:T(2,128)(2,1)} copy(bf16[32,2,2,5120]{3,0,2,1:T(8,128)(2,1)} %reduce-scatter.2.cloned.1.call-done) | data formatting | bytes 2621440 | tf_op jit(solution)/shard_map/reduce_scatter | solution.py:156
  (40 shorter events, 0.4 us)
Async XLA Ops:
  6.5 242.0 %reduce-scatter.2.cloned.1.call-start = ((), (), s32[]{:S(2)}) async-start(), calls=%async_computation.1 | async-start | bytes 3932160 | tf_op jit(solution)/shard_map/reduce_scatter | solution.py:156
  6.5 17.9 %collective-permute-start = (bf16[2,2,2,64,640]{4,3,2,1,0:T(8,128)(2,1)}, bf16[2,2,2,64,640]{4,3,2,1,0:T(8,128)(2,1)S(1)}, u32[]{:S(2)}, u32[]{:S(2)}) collective-permute-start(bf16[2,2,2,64,640]{4,3,2,1,0:T(8,128)(2,1)} %param.4), channel_id=1, source_target_pairs={{0,2},{2,0},{4,6},{6,4},{8,10},{10,8},{12,14},{14,12},{1,3},{3,1},... | collective-permute-start | bytes 1966088 | tf_op jit(solution)/shard_map/ppermute | solution.py:93
  26.0 1.9 copy-start.1
  26.0 30.1 %collective-permute-start.1 = (bf16[2,2,4,64,640]{4,3,2,1,0:T(8,128)(2,1)S(1)}, bf16[2,2,4,64,640]{4,3,2,1,0:T(8,128)(2,1)}, u32[]{:S(2)}, u32[]{:S(2)}) collective-permute-start(bf16[2,2,4,64,640]{4,3,2,1,0:T(8,128)(2,1)S(1)} %maximum_select_fusion.2), channel_id=1, source_target_pairs={{0,4},{2,6},{4,0},{6,2},{8,12},{10,14},{12,8},{14,10},{1,5},{3,7},... | collective-permute-start | bytes 3932168 | tf_op jit(solution)/shard_map/ppermute | solution.py:93
  59.1 114.4 %collective-permute-start.2 = (bf16[2,2,8,64,640]{4,3,2,1,0:T(8,128)(2,1)S(1)}, bf16[2,2,8,64,640]{4,3,2,1,0:T(8,128)(2,1)}, u32[]{:S(2)}, u32[]{:S(2)}) collective-permute-start(bf16[2,2,8,64,640]{4,3,2,1,0:T(8,128)(2,1)S(1)} %maximum_select_fusion.1), channel_id=1, source_target_pairs={{0,8},{2,10},{4,12},{6,14},{8,0},{10,2},{12,4},{14,6},{1,9},{3,11}... | collective-permute-start | bytes 7864328 | tf_op jit(solution)/shard_map/ppermute | solution.py:93
  177.5 3.2 %copy-start = (bf16[2,2,16,64,640]{4,3,2,1,0:T(8,128)(2,1)}, bf16[2,2,16,64,640]{4,3,2,1,0:T(8,128)(2,1)S(1)}, u32[]{:S(2)}) copy-start(bf16[2,2,16,64,640]{4,3,2,1,0:T(8,128)(2,1)S(1)} %maximum_select_fusion) | copy-start | bytes 15728644
  180.8 5.3 %collective-permute-start.3 = (bf16[2,1,16,64,640]{4,3,2,1,0:T(8,128)(2,1)}, bf16[2,1,16,64,640]{4,3,2,1,0:T(8,128)(2,1)}, u32[]{:S(2)}, u32[]{:S(2)}) collective-permute-start(bf16[2,1,16,64,640]{4,3,2,1,0:T(8,128)(2,1)} %constant_dynamic-slice_fusion), channel_id=1, source_target_pairs={{0,16},{16,0},{1,17},{17,1},{2,18},{18,2},{3,19},{19,3},{4,20},{20... | collective-permute-start | bytes 7864328 | tf_op jit(solution)/shard_map/ppermute | solution.py:18
  183.3 2.1 copy-start.2
  202.9 2.6 slice-start
  203.9 2.2 slice-start.1
Sparse Core Ops, SparseCore 0:
  210.0 38.4 reduce-scatter.1
